TPU v7x, 32 devices: a whole 2x2x4 slice. The times are simulated.
32 devices in a mesh: shard: 4 (over x, core), ctx: 4 (over z), tp: 2 (over y).
Axes of the slice: x: 2, y: 2, z: 4, core: 2. Of those that a mesh axis runs over, the one named last changes fastest.
Arguments:
- tokens: bfloat16 [10240, 1024], P(('shard', 'ctx')), may hold values from -6 to 6
- cotangent: bfloat16 [10240, 1024], P(('shard', 'ctx')), may hold values from -6 to 6
- seg_ids: int32 [10240], P(('shard', 'ctx')), may hold values from 0 to 51, as said below
- positions: int32 [10240], P(('shard', 'ctx')), may hold values from 0 to 1279, as said below
- parents: int32 [52], replicated, may hold values from 0 to 51, as said below
- w_qkv: bfloat16 [3, 1024, 1024], P(None, ('shard', 'ctx'), 'tp'), may hold values from -0.1875 to 0.1875
- b_qv: float32 [2, 1024], P(None, 'tp'), may hold values from -4 to 4
- w_out: bfloat16 [1024, 1024], P('tp', ('shard', 'ctx')), may hold values from -0.5 to 0.5
- b_out: float32 [1024], replicated, may hold values from -4 to 4
- w_up: bfloat16 [1024, 4096], P(('shard', 'ctx'), 'tp'), may hold values from -0.1875 to 0.1875
- b_up: float32 [4096], P('tp'), may hold values from -4 to 4
- w_down: bfloat16 [4096, 1024], P('tp', ('shard', 'ctx')), may hold values from -0.09375 to 0.09375
- b_down: float32 [1024], replicated, may hold values from -4 to 4
- ln_gain: float32 [2, 1024], replicated, may hold values from 0.5 to 1.5
- ln_bias: float32 [2, 1024], replicated, may hold values from -3 to 3
Outputs:
- result: bfloat16 [10240, 1024], P(('shard', 'ctx'))
- grad_tokens: float32 [10240, 1024], P(('shard', 'ctx'))
- grad_w_qkv: float32 [3, 1024, 1024], P(None, ('shard', 'ctx'), 'tp')
- grad_b_qv: float32 [2, 1024], P(None, 'tp')
- grad_w_out: float32 [1024, 1024], P('tp', ('shard', 'ctx'))
- grad_b_out: float32 [1024], replicated
- grad_w_up: float32 [1024, 4096], P(('shard', 'ctx'), 'tp')
- grad_b_up: float32 [4096], P('tp')
- grad_w_down: float32 [4096, 1024], P('tp', ('shard', 'ctx'))
- grad_b_down: float32 [1024], replicated
- grad_ln_gain: float32 [2, 1024], replicated
- grad_ln_bias: float32 [2, 1024], replicated
Inputs may be any that keep to these rules, and one draw needn't show every extreme that they name: `seg_ids`: each aligned run of 2560 tokens is one tree of 13 segments: a trunk of 1024 tokens first, then 4 branches and 8 leaves of 128 tokens each, each segment's tokens adjacent and after its parent's; every segment number labels exactly one segment. Positions count from 0 at the trunk's start along the path; a segment's tokens have consecutive positions following its parent's last. `parents`: A trunk is its own parent; a branch's parent is its trunk, a leaf's parent a branch of its tree, each branch parent of two leaves.
All inputs are finite; a program needn't handle non-finite values.
Results may differ from a plain program's by a relative error of at most 0.015.
Values may be sent and summed in bfloat16 or wider, within the bound.
A program may use at most 192 MiB of HBM per device.

v0:
```python
from functools import partial
import jax
import jax.numpy as jnp
from jax import lax
from jax.sharding import PartitionSpec as P

HEADS = 16
HD = 64
KEY_BLOCK = 512
EPS = 1e-05
NEG = -1e30


def norm_forward(inputs_in, gain_row, shift_row):
    centre = inputs_in - jnp.mean(inputs_in, axis=-1, keepdims=True)
    inverse = lax.rsqrt(jnp.mean(centre * centre, axis=-1, keepdims=True) + EPS)
    normed = centre * inverse
    return (normed * gain_row + shift_row, normed, inverse)


def norm_backward(grad_in, normed, inverse, gain_row):
    scaled = grad_in * gain_row
    mean_grad = jnp.mean(scaled, axis=-1, keepdims=True)
    mean_cross = jnp.mean(scaled * normed, axis=-1, keepdims=True)
    return inverse * (scaled - mean_grad - normed * mean_cross)


def ancestry(seg_vals, parents):
    first_up = jnp.take(parents, seg_vals)
    return (first_up, jnp.take(parents, first_up))


def block_scores(query_heads, key_heads, query_tags, key_tags, slopes):
    q_seg, q_first, q_second, q_pos = query_tags
    k_seg, k_pos = key_tags
    raw_scores = jnp.einsum(
        "qhd,khd->hqk", query_heads, key_heads, preferred_element_type=jnp.float32
    ) * HD ** (-0.5)
    distance = (q_pos[:, None] - k_pos[None, :]).astype(jnp.float32)
    scores = raw_scores - slopes[:, None, None] * distance[None]
    related = (
        (k_seg[None, :] == q_seg[:, None])
        | (k_seg[None, :] == q_first[:, None])
        | (k_seg[None, :] == q_second[:, None])
    )
    allowed = related & (k_pos[None, :] <= q_pos[:, None])
    return (scores, allowed[None])


def probabilities(scores, allowed, row_max, row_sum):
    shifted = jnp.where(allowed, scores - row_max[:, :, None], NEG)
    return jnp.exp(shifted) / row_sum[:, :, None]


def per_device(
    tokens,
    cotangent,
    seg_ids,
    positions,
    parents,
    w_qkv,
    b_qv,
    w_out,
    b_out,
    w_up,
    b_up,
    w_down,
    b_down,
    ln_gain,
    ln_bias,
):
    num_rows = tokens.shape[0]
    head_count = HEADS // lax.axis_size("tp")
    head_width = head_count * HD
    head_index = (lax.axis_index("tp") * head_count + jnp.arange(head_count)).astype(jnp.float32)
    slopes = 2.0 ** (-8.0 * (head_index + 1.0) / HEADS)
    scale = HD ** (-0.5)
    full_qkv, full_out = (
        lax.all_gather(w_qkv, ("shard", "ctx"), axis=1, tiled=True),
        lax.all_gather(w_out, ("shard", "ctx"), axis=1, tiled=True),
    )
    group_seg, group_pos = (
        lax.all_gather(seg_ids, "ctx", axis=0, tiled=True),
        lax.all_gather(positions, "ctx", axis=0, tiled=True),
    )
    own_first, own_second = ancestry(seg_ids, parents)
    own_tags = (seg_ids, own_first, own_second, positions)
    inputs = tokens.astype(jnp.float32)
    norm_one, normed_one, inverse_one = norm_forward(inputs, ln_gain[0], ln_bias[0])
    act_one = norm_one.astype(jnp.bfloat16)
    projected = jnp.einsum("td,cde->cte", act_one, full_qkv, preferred_element_type=jnp.float32)
    qkv_bias = jnp.stack([b_qv[0], jnp.zeros((head_width,), jnp.float32), b_qv[1]])
    qkv_low = (projected + qkv_bias[:, None, :]).astype(jnp.bfloat16)
    query_flat, key_flat, value_flat = (qkv_low[0], qkv_low[1], qkv_low[2])
    group_keys, group_values = (
        lax.all_gather(key_flat, "ctx", axis=0, tiled=True),
        lax.all_gather(value_flat, "ctx", axis=0, tiled=True),
    )
    group_rows = group_keys.shape[0]
    block_count = group_rows // KEY_BLOCK
    key_blocks = group_keys.reshape(block_count, KEY_BLOCK, head_count, HD)
    value_blocks = group_values.reshape(block_count, KEY_BLOCK, head_count, HD)
    seg_blocks = group_seg.reshape(block_count, KEY_BLOCK)
    pos_blocks = group_pos.reshape(block_count, KEY_BLOCK)
    query_heads = query_flat.reshape(num_rows, head_count, HD)

    def stats_step(carry_in, block_parts):
        row_max, row_sum = carry_in
        key_part, seg_part, pos_part = block_parts
        scores, allowed = block_scores(
            query_heads, key_part, own_tags, (seg_part, pos_part), slopes
        )
        new_max = jnp.maximum(row_max, jnp.max(jnp.where(allowed, scores, NEG), axis=-1))
        shifted = jnp.where(allowed, scores - new_max[:, :, None], NEG)
        row_sum = row_sum * jnp.exp(row_max - new_max) + jnp.sum(jnp.exp(shifted), axis=-1)
        return ((new_max, row_sum), None)

    start_stats = (
        jnp.full((head_count, num_rows), NEG, jnp.float32),
        jnp.zeros((head_count, num_rows), jnp.float32),
    )
    (row_max, row_sum), _ = lax.scan(stats_step, start_stats, (key_blocks, seg_blocks, pos_blocks))

    def output_step(out_accum, block_parts):
        key_part, value_part, seg_part, pos_part = block_parts
        scores, allowed = block_scores(
            query_heads, key_part, own_tags, (seg_part, pos_part), slopes
        )
        prob_low = probabilities(scores, allowed, row_max, row_sum).astype(jnp.bfloat16)
        return (
            out_accum
            + jnp.einsum("hqk,khd->qhd", prob_low, value_part, preferred_element_type=jnp.float32),
            None,
        )

    attended, _ = lax.scan(
        output_step,
        jnp.zeros((num_rows, head_count, HD), jnp.float32),
        (key_blocks, value_blocks, seg_blocks, pos_blocks),
    )
    attended_low = attended.reshape(num_rows, head_width).astype(jnp.bfloat16)
    branch_one = (
        lax.psum(
            jnp.dot(attended_low, full_out, preferred_element_type=jnp.float32).astype(
                jnp.bfloat16
            ),
            "tp",
        ).astype(jnp.float32)
        + b_out
    )
    middle = inputs + branch_one
    full_up, full_down = (
        lax.all_gather(w_up, ("shard", "ctx"), axis=0, tiled=True),
        lax.all_gather(w_down, ("shard", "ctx"), axis=1, tiled=True),
    )
    norm_two, normed_two, inverse_two = norm_forward(middle, ln_gain[1], ln_bias[1])
    act_two = norm_two.astype(jnp.bfloat16)
    upper_in = jnp.dot(act_two, full_up, preferred_element_type=jnp.float32) + b_up
    gelu_vals, gelu_pull = jax.vjp(partial(jax.nn.gelu, approximate=True), upper_in)
    hidden = gelu_vals.astype(jnp.bfloat16)
    branch_two = (
        lax.psum(
            jnp.dot(hidden, full_down, preferred_element_type=jnp.float32).astype(jnp.bfloat16),
            "tp",
        ).astype(jnp.float32)
        + b_down
    )
    result = (middle + branch_two).astype(jnp.bfloat16)
    grad_out = cotangent.astype(jnp.float32)
    grad_hidden = jnp.einsum("td,fd->tf", cotangent, full_down, preferred_element_type=jnp.float32)
    grad_upper = gelu_pull(grad_hidden)[0].astype(jnp.bfloat16)
    down_term = jnp.einsum("tf,td->fd", hidden, cotangent, preferred_element_type=jnp.float32)
    up_term = jnp.einsum("td,tf->df", act_two, grad_upper, preferred_element_type=jnp.float32)
    grad_w_up, grad_w_down = (
        lax.psum_scatter(up_term, ("shard", "ctx"), scatter_dimension=0, tiled=True),
        lax.psum_scatter(down_term, ("shard", "ctx"), scatter_dimension=1, tiled=True),
    )
    grad_norm_two = lax.psum(
        jnp.einsum("tf,df->td", grad_upper, full_up, preferred_element_type=jnp.float32).astype(
            jnp.bfloat16
        ),
        "tp",
    ).astype(jnp.float32)
    grad_middle = grad_out + norm_backward(grad_norm_two, normed_two, inverse_two, ln_gain[1])
    grad_branch = grad_middle.astype(jnp.bfloat16)
    out_term = jnp.einsum(
        "te,td->ed", attended_low, grad_branch, preferred_element_type=jnp.float32
    )
    grad_att = jnp.einsum(
        "td,ed->te", grad_branch, full_out, preferred_element_type=jnp.float32
    ).astype(jnp.bfloat16)
    grad_heads = grad_att.reshape(num_rows, head_count, HD)
    row_terms = jnp.einsum("qhd,qhd->hq", grad_heads.astype(jnp.float32), attended)

    def joint_step(grad_accum, block_parts):
        key_part, value_part, seg_part, pos_part = block_parts
        scores, allowed = block_scores(
            query_heads, key_part, own_tags, (seg_part, pos_part), slopes
        )
        prob_vals = probabilities(scores, allowed, row_max, row_sum)
        grad_probs = jnp.einsum(
            "qhd,khd->hqk", grad_heads, value_part, preferred_element_type=jnp.float32
        )
        grad_scores = (prob_vals * (grad_probs - row_terms[:, :, None])).astype(jnp.bfloat16)
        grad_accum = (
            grad_accum
            + jnp.einsum("hqk,khd->qhd", grad_scores, key_part, preferred_element_type=jnp.float32)
            * scale
        )
        key_part_grad = (
            jnp.einsum("hqk,qhd->khd", grad_scores, query_heads, preferred_element_type=jnp.float32)
            * scale
        )
        value_part_grad = jnp.einsum(
            "hqk,qhd->khd",
            prob_vals.astype(jnp.bfloat16),
            grad_heads,
            preferred_element_type=jnp.float32,
        )
        return (
            grad_accum,
            (
                key_part_grad.reshape(KEY_BLOCK, head_width),
                value_part_grad.reshape(KEY_BLOCK, head_width),
            ),
        )

    grad_query_sum, (key_terms, value_terms) = lax.scan(
        joint_step,
        jnp.zeros((num_rows, head_count, HD), jnp.float32),
        (key_blocks, value_blocks, seg_blocks, pos_blocks),
    )
    key_grad_sum, value_grad_sum = (
        lax.psum_scatter(
            key_terms.reshape(group_rows, head_width).astype(jnp.bfloat16),
            "ctx",
            scatter_dimension=0,
            tiled=True,
        ).astype(jnp.float32),
        lax.psum_scatter(
            value_terms.reshape(group_rows, head_width).astype(jnp.bfloat16),
            "ctx",
            scatter_dimension=0,
            tiled=True,
        ).astype(jnp.float32),
    )
    grad_query_low = grad_query_sum.reshape(num_rows, head_width).astype(jnp.bfloat16)
    grad_key_low = key_grad_sum.astype(jnp.bfloat16)
    grad_value_low = value_grad_sum.astype(jnp.bfloat16)
    grad_qkv = jnp.stack([grad_query_low, grad_key_low, grad_value_low])
    grad_norm_one = lax.psum(
        jnp.einsum("cte,cde->td", grad_qkv, full_qkv, preferred_element_type=jnp.float32).astype(
            jnp.bfloat16
        ),
        "tp",
    ).astype(jnp.float32)
    grad_tokens = grad_middle + norm_backward(grad_norm_one, normed_one, inverse_one, ln_gain[0])
    qkv_term = jnp.einsum("td,cte->cde", act_one, grad_qkv, preferred_element_type=jnp.float32)
    grad_w_qkv, grad_w_out = (
        lax.psum_scatter(qkv_term, ("shard", "ctx"), scatter_dimension=1, tiled=True),
        lax.psum_scatter(out_term, ("shard", "ctx"), scatter_dimension=1, tiled=True),
    )
    bias_qv_part = jnp.stack(
        [
            jnp.sum(grad_query_low.astype(jnp.float32), axis=0),
            jnp.sum(grad_value_low.astype(jnp.float32), axis=0),
        ]
    )
    out_bias_part = jnp.sum(grad_branch.astype(jnp.float32), axis=0)
    up_bias_part = jnp.sum(grad_upper.astype(jnp.float32), axis=0)
    down_bias_part = jnp.sum(grad_out, axis=0)
    gain_part = jnp.stack(
        [jnp.sum(grad_norm_one * normed_one, axis=0), jnp.sum(grad_norm_two * normed_two, axis=0)]
    )
    shift_part = jnp.stack([jnp.sum(grad_norm_one, axis=0), jnp.sum(grad_norm_two, axis=0)])
    grad_b_qv, grad_b_out, grad_b_up, grad_b_down, grad_gain, grad_shift = lax.psum(
        (bias_qv_part, out_bias_part, up_bias_part, down_bias_part, gain_part, shift_part),
        ("shard", "ctx"),
    )
    return (
        result,
        grad_tokens,
        grad_w_qkv,
        grad_b_qv,
        grad_w_out,
        grad_b_out,
        grad_w_up,
        grad_b_up,
        grad_w_down,
        grad_b_down,
        grad_gain,
        grad_shift,
    )


def solution(mesh):
    placed = (
        P(("shard", "ctx"), None),
        P(("shard", "ctx"), None),
        P(("shard", "ctx")),
        P(("shard", "ctx")),
        P(),
        P(None, ("shard", "ctx"), "tp"),
        P(None, "tp"),
        P("tp", ("shard", "ctx")),
        P(),
        P(("shard", "ctx"), "tp"),
        P("tp"),
        P("tp", ("shard", "ctx")),
        P(),
        P(),
        P(),
    )
    return jax.shard_map(
        per_device,
        mesh=mesh,
        in_specs=placed,
        out_specs=(
            P(("shard", "ctx"), None),
            P(("shard", "ctx"), None),
            P(None, ("shard", "ctx"), "tp"),
            P(None, "tp"),
            P("tp", ("shard", "ctx")),
            P(),
            P(("shard", "ctx"), "tp"),
            P("tp"),
            P("tp", ("shard", "ctx")),
            P(),
            P(),
            P(),
        ),
        check_vma=False,
    )
```

profile of v0, /device:TPU:0, one launch (start us, length us, event | category | flops | bytes accessed | tf_op | source)
XLA Modules:
  0.0 1227.4 jit_solution(17177384141970764091)
XLA Ops:
  11.7 46.8 %all-gather.11.cloned.1.call-done = bf16[3,1024,512]{2,1,0:T(8,128)(2,1)} async-done(((bf16[3,64,512]{2,1,0:T(8,128)(2,1)}), bf16[3,1024,512]{2,1,0:T(8,128)(2,1)}) %all-gather.11.cloned.1.call-update) | async-done | bytes 3145744 | tf_op jit(solution)/shard_map/all_gather | solution.py:79
  58.5 4.7 fusion.83
  68.2 13.2 %all-gather.2 = s32[4,1,640]{2,1,0:T(1,128)S(1)} all-gather(s32[1,1,640]{2,1,0:T(1,128)S(1)} %reshape.676), channel_id=1, replica_groups=mesh['shard'=4,'ctx'=4,'tp'=2] {'ctx'}, dimensions={0}, use_global_device_ids=true | all-gather | bytes 12800 | tf_op jit(solution)/shard_map/all_gather | solution.py:83
  81.5 13.3 %all-gather.3 = s32[4,1,640]{2,1,0:T(1,128)S(1)} all-gather(s32[1,1,640]{2,1,0:T(1,128)S(1)} %reshape.678), channel_id=1, replica_groups=mesh['shard'=4,'ctx'=4,'tp'=2] {'ctx'}, dimensions={0}, use_global_device_ids=true | all-gather | bytes 12800 | tf_op jit(solution)/shard_map/all_gather | solution.py:84
  94.9 32.4 %select_select_fusion = (s32[640]{0:T(1024)S(1)}, s32[640]{0:T(1024)S(1)}) fusion(s32[]{:T(128)} %bitcast.57, s32[]{:T(128)} %bitcast.56, s32[]{:T(128)} %bitcast.55, s32[]{:T(128)} %bitcast.54, s32[]{:T(128)} %bitcast.53, s32[]{:T(128)} %bitcast.52, s32[]{:T(128)} %bitcast.51, s32[]{:T(128)} %bitcast.50, s32[]{:T(128)} %bitcast.49, s32[]{:T(128)} %bitcast.48, ...), kind=kLoop, calls=%fused_computation.139 | loop fusion | flops 139520 | bytes 7888 | tf_op jit(solution)/shard_map/jit(_take)/select_n | solution.py:30
  127.3 7.1 reshape.547
  134.4 4.7 copy.60
  139.0 34.5 %all-gather.21.cloned.1.call-done = bf16[1,2560,512]{1,2,0:T(8,128)(2,1)} async-done(((bf16[1,640,512]{1,2,0:T(8,128)(2,1)}), bf16[1,2560,512]{1,2,0:T(8,128)(2,1)}) %all-gather.21.cloned.1.call-update) | async-done | bytes 2621456 | tf_op jit(solution)/shard_map/all_gather | solution.py:96
  173.6 7.0 reshape.550
  180.6 4.7 copy.61
  185.3 41.6 %while.39 = (s32[]{:T(128)}, f32[8,640]{1,0:T(8,128)S(1)}, f32[8,640]{1,0:T(8,128)S(1)}, s32[5,512]{1,0:T(8,128)S(1)}, s32[640]{0:T(1024)S(1)}, /*index=5*/s32[6...) while((s32[]{:T(128)}, f32[8,640]{1,0:T(8,128)S(1)}, ...), condition=%wide.region_5.7_spmd.clone, body=%wide.region_2.6_spmd.clone.sunk | while | flops 367354912 | bytes 27360004 | solution.py:122
  185.9 4.7 select_reduce_fusion.2
  194.2 4.7 select_reduce_fusion.2
  202.6 4.8 select_reduce_fusion.2
  210.9 4.8 select_reduce_fusion.2
  219.2 4.8 select_reduce_fusion.2
  226.9 40.9 %while.40 = (s32[]{:T(128)}, f32[640,8,64]{0,2,1:T(8,128)}, bf16[5,512,8,64]{1,3,2,0:T(8,128)(2,1)}, s32[5,512]{1,0:T(8,128)S(1)}, s32[640]{0:T(1024)S(1)}, /*in...) while((s32[]{:T(128)}, f32[640,8,64]{0,2,1:T(8,128)}, ...), condition=%wide.region_7.9_spmd.clone, body=%wide.region_6.8_spmd.clone.sunk | while | flops 693043264 | bytes 7672046 | solution.py:136
  227.8 7.2 fusion.154
  235.6 7.6 fusion.154
  243.8 7.6 fusion.154
  252.0 7.6 fusion.154
  260.2 7.6 fusion.154
  274.1 43.2 %all-reduce.8.cloned.1.call-done = bf16[640,1024]{1,0:T(8,128)(2,1)} async-done(((bf16[640,1024]{1,0:T(8,128)(2,1)}), bf16[640,1024]{1,0:T(8,128)(2,1)}) %all-reduce.8.cloned.1.call-update) | async-done | bytes 1310736 | tf_op jit(solution)/shard_map/psum | solution.py:143
  319.9 50.4 %all-gather.15.cloned.1.call-done = bf16[1024,2048]{1,0:T(8,128)(2,1)} async-done(((bf16[64,2048]{1,0:T(8,128)(2,1)}), bf16[1024,2048]{1,0:T(8,128)(2,1)}) %all-gather.15.cloned.1.call-update) | async-done | bytes 4194320 | tf_op jit(solution)/shard_map/all_gather | solution.py:153
  370.3 7.7 fusion.95
  378.1 43.8 %all-gather.17.cloned.1.call-done = bf16[2048,1024]{0,1:T(8,128)(2,1)} async-done(((bf16[2048,64]{0,1:T(8,128)(2,1)}), bf16[2048,1024]{0,1:T(8,128)(2,1)}) %all-gather.17.cloned.1.call-update) | async-done | bytes 4194320 | tf_op jit(solution)/shard_map/all_gather | solution.py:154
  421.9 9.6 convert_reduce_fusion
  437.1 44.3 %all-reduce.10.cloned.1.call-done = bf16[640,1024]{1,0:T(8,128)(2,1)} async-done(((bf16[640,1024]{1,0:T(8,128)(2,1)}), bf16[640,1024]{1,0:T(8,128)(2,1)}) %all-reduce.10.cloned.1.call-update) | async-done | bytes 1310736 | tf_op jit(solution)/shard_map/psum | solution.py:178
  489.5 80.2 %while.41 = (s32[]{:T(128)}, f32[640,8,64]{0,2,1:T(8,128)S(1)}, bf16[5,512,512]{1,2,0:T(8,128)(2,1)}, bf16[5,512,512]{1,2,0:T(8,128)(2,1)}, bf16[5,512,8,64]{1,3...) while((s32[]{:T(128)}, f32[640,8,64]{0,2,1:T(8,128)S(1)}, ...), condition=%wide.region_16.18_spmd.clone, body=%wide.region_15.17_spmd.clone.sunk | while | flops 1708392448 | bytes 60513056 | solution.py:228
  490.1 5.1 fusion.165
  506.1 5.1 fusion.165
  522.2 5.1 fusion.165
  538.2 5.1 fusion.165
  554.3 5.1 fusion.165
  579.3 8.7 convolution_convert_fusion.1
  588.4 37.9 %reduce-scatter.8.cloned.1.call-done = bf16[640,512]{1,0:T(8,128)(2,1)} async-done(((bf16[2560,512]{1,0:T(8,128)(2,1)}), bf16[640,512]{1,0:T(8,128)(2,1)}) %reduce-scatter.8.cloned.1.call-update) | async-done | bytes 655376 | tf_op jit(solution)/shard_map/reduce_scatter | solution.py:240
  626.4 54.0 %reduce-scatter.6.cloned.1.call-done = bf16[640,512]{1,0:T(8,128)(2,1)} async-done(((bf16[2560,512]{1,0:T(8,128)(2,1)}), bf16[640,512]{1,0:T(8,128)(2,1)}) %reduce-scatter.6.cloned.1.call-update) | async-done | bytes 655376 | tf_op jit(solution)/shard_map/reduce_scatter | solution.py:234
  680.4 5.6 bitcast_convert_fusion
  687.5 5.8 convolution_bitcast_fusion
  693.3 9.5 copy.68
  708.0 9.7 fusion.96
  719.1 7.8 fusion.94
  729.0 31.5 %all-reduce.14.cloned.1.call-done = (bf16[640,1024]{1,0:T(8,128)(2,1)}, bf16[640,1024]{1,0:T(8,128)(2,1)}) async-done(((bf16[640,1024]{1,0:T(8,128)(2,1)}, bf16[640,1024]{1,0:T(8,128)(2,1)}), (bf16[640,1024]{1,0:T(8,128)(2,1)}, bf16[640,1024]{1,0:T(8,128)(2,1)})) %all-reduce.14.cloned.1.call-update) | async-done | bytes 2621456 | tf_op jit(solution)/shard_map/psum | solution.py:162
  763.0 65.9 %all-reduce.1 = (f32[2,512]{1,0:T(2,128)}, f32[1024]{0:T(1024)}, f32[2048]{0:T(1024)}, f32[1024]{0:T(1024)}, f32[2,1024]{1,0:T(2,128)}, /*index=5*/f32[2,1024]{1,0:T(2,128)}) all-reduce(f32[2,512]{1,0:T(2,128)S(1)} %pad_maximum_fusion.6, f32[1024]{0:T(1024)S(1)} %copy-done.32, ...), channel_id=1, replica_groups=mesh['shard'=4,'ctx'=4,'tp'=2] {'shard','ctx'}, use_global_device_ids=true, to_apply=%region_25.27 | all-reduce | flops 9216 | bytes 73728 | tf_op jit(solution)/shard_map/psum | solution.py:276
  833.4 103.3 %all-reduce.12.cloned.1.call-done = f32[3,1024,512]{2,0,1:T(4,128)} async-done(((f32[3,1024,512]{2,0,1:T(4,128)}), f32[3,1024,512]{2,0,1:T(4,128)}) %all-reduce.12.cloned.1.call-update) | async-done | bytes 6291472
  938.7 63.8 %reduce-scatter.10.cloned.1.call-done = f32[512,64]{0,1:T(8,128)} async-done(((f32[512,1024]{0,1:T(8,128)}), f32[512,64]{0,1:T(8,128)}) %reduce-scatter.10.cloned.1.call-update) | async-done | bytes 131088 | tf_op jit(solution)/shard_map/reduce_scatter | solution.py:261
  1002.5 108.7 %reduce-scatter.14.cloned.1.call-done = f32[2048,64]{0,1:T(8,128)} async-done(((f32[2048,1024]{0,1:T(8,128)}), f32[2048,64]{0,1:T(8,128)}) %reduce-scatter.14.cloned.1.call-update) | async-done | bytes 524304 | tf_op jit(solution)/shard_map/reduce_scatter | solution.py:176
  1111.2 109.4 %reduce-scatter.12.cloned.1.call-done = f32[64,2048]{1,0:T(8,128)} async-done(((f32[1024,2048]{1,0:T(8,128)}), f32[64,2048]{1,0:T(8,128)}) %reduce-scatter.12.cloned.1.call-update) | async-done | bytes 524304 | tf_op jit(solution)/shard_map/reduce_scatter | solution.py:175
  (297 shorter events, 135.1 us)
Async XLA Ops:
  7.2 51.3 %copy-start = (bf16[640,1024]{1,0:T(8,128)(2,1)S(1)}, bf16[640,1024]{1,0:T(8,128)(2,1)}, u32[]{:S(2)}) copy-start(bf16[640,1024]{1,0:T(8,128)(2,1)} %param.23) | copy-start | bytes 3932164
  7.2 4.3 copy-start.40
  7.2 4.4 copy-start.36
  7.2 4.4 copy-start.37
  7.2 51.2 %all-gather.11.cloned.1.call-start = ((), (), s32[]{:S(2)}) async-start(), calls=%async_computation.5 | async-start | bytes 3342336 | tf_op jit(solution)/shard_map/all_gather | solution.py:79
  8.0 119.3 %all-gather.19.cloned.1.call-start = ((), (), s32[]{:S(2)}) async-start(), calls=%async_computation.16 | async-start | bytes 3276800 | tf_op jit(solution)/shard_map/all_gather | solution.py:97
  9.6 48.8 %copy-start.20 = (f32[640]{0:T(1024)}, f32[640]{0:T(1024)S(1)}, u32[]{:S(2)}) copy-start(f32[640]{0:T(1024)S(1)} %broadcast_multiply_fusion.5) | copy-start | bytes 7684
  11.5 51.7 %copy-start.24 = (f32[640]{0:T(1024)}, f32[640]{0:T(1024)S(1)}, u32[]{:S(2)}) copy-start(f32[640]{0:T(1024)S(1)} %add_rsqrt_fusion.1) | copy-start | bytes 7684
  11.6 51.6 %copy-start.26 = (f32[1,1024]{1,0:T(1,128)}, f32[1,1024]{1,0:T(1,128)S(1)}, u32[]{:S(2)}) copy-start(f32[1,1024]{1,0:T(1,128)S(1)} %get-tuple-element.692) | copy-start | bytes 12292
  11.6 473.8 %copy-start.30 = (f32[1,1024]{1,0:T(1,128)}, f32[1,1024]{1,0:T(1,128)S(1)}, u32[]{:S(2)}) copy-start(f32[1,1024]{1,0:T(1,128)S(1)} %get-tuple-element.693) | copy-start | bytes 12292
  11.6 51.6 %copy-start.43 = (f32[1,1024]{1,0:T(1,128)}, f32[1,1024]{1,0:T(1,128)S(1)}, u32[]{:S(2)}) copy-start(f32[1,1024]{1,0:T(1,128)S(1)} %get-tuple-element.694) | copy-start | bytes 12292
  11.6 358.7 %copy-start.41 = (f32[1,1024]{1,0:T(1,128)}, f32[1,1024]{1,0:T(1,128)S(1)}, u32[]{:S(2)}) copy-start(f32[1,1024]{1,0:T(1,128)S(1)} %get-tuple-element.695) | copy-start | bytes 12292
  63.2 2.8 copy-start.11
  63.2 4.9 copy-start.8
  63.3 4.9 copy-start.14
  64.6 108.9 %all-gather.21.cloned.1.call-start = ((), (), s32[]{:S(2)}) async-start(), calls=%async_computation.17 | async-start | bytes 3276800 | tf_op jit(solution)/shard_map/all_gather | solution.py:96
  65.4 203.9 %all-gather.13.cloned.1.call-start = ((), (), s32[]{:S(2)}) async-start(), calls=%async_computation.6 | async-start | bytes 1114112 | tf_op jit(solution)/shard_map/all_gather | solution.py:80
  65.9 251.4 %all-reduce.8.cloned.1.call-start = ((), (), s32[]{:S(2)}) async-start(), calls=%async_computation.7 | async-start | bytes 2621440 | tf_op jit(solution)/shard_map/psum | solution.py:143
  269.3 4.1 copy-start.9
  269.3 48.0 %copy-start.18 = (f32[1024]{0:T(1024)S(1)}, f32[1024]{0:T(1024)}, u32[]{:S(2)}) copy-start(f32[1024]{0:T(1024)} %param.31) | copy-start | bytes 12292
  272.7 97.6 %all-gather.15.cloned.1.call-start = ((), (), s32[]{:S(2)}) async-start(), calls=%async_computation.8 | async-start | bytes 4456448 | tf_op jit(solution)/shard_map/all_gather | solution.py:153
  273.3 148.5 %all-gather.17.cloned.1.call-start = ((), (), s32[]{:S(2)}) async-start(), calls=%async_computation.9 | async-start | bytes 4456448 | tf_op jit(solution)/shard_map/all_gather | solution.py:154
  274.1 207.3 %all-reduce.10.cloned.1.call-start = ((), (), s32[]{:S(2)}) async-start(), calls=%async_computation.10 | async-start | bytes 2621440 | tf_op jit(solution)/shard_map/psum | solution.py:178
  319.2 166.1 %copy-start.22 = (f32[640]{0:T(1024)}, f32[640]{0:T(1024)S(1)}, u32[]{:S(2)}) copy-start(f32[640]{0:T(1024)S(1)} %broadcast_multiply_fusion.4) | copy-start | bytes 7684
  319.9 165.5 %copy-start.28 = (f32[640]{0:T(1024)}, f32[640]{0:T(1024)S(1)}, u32[]{:S(2)}) copy-start(f32[640]{0:T(1024)S(1)} %add_rsqrt_fusion) | copy-start | bytes 7684
  370.3 51.5 %copy-start.47 = (f32[2048]{0:T(1024)S(1)}, f32[2048]{0:T(1024)}, u32[]{:S(2)}) copy-start(f32[2048]{0:T(1024)} %param.33) | copy-start | bytes 24580
  421.9 11.1 copy-start.45
  437.0 189.4 %reduce-scatter.8.cloned.1.call-start = ((), (), s32[]{:S(2)}) async-start(), calls=%async_computation.12 | async-start | bytes 3276800 | tf_op jit(solution)/shard_map/reduce_scatter | solution.py:240
  481.4 4.0 copy-start.4
  481.4 4.0 copy-start.7
  481.4 4.0 copy-start.12
  485.4 2.6 copy-start.6
  485.4 2.5 copy-start.15
  574.1 106.2 %reduce-scatter.6.cloned.1.call-start = ((), (), s32[]{:S(2)}) async-start(), calls=%async_computation.11 | async-start | bytes 3276800 | tf_op jit(solution)/shard_map/reduce_scatter | solution.py:234
  578.6 181.8 %all-reduce.14.cloned.1.call-start = ((), (), s32[]{:S(2)}) async-start(), calls=%async_computation.19 | async-start | bytes 5242880 | tf_op jit(solution)/shard_map/psum | solution.py:162
  680.4 5.8 copy-start.46
  686.1 250.7 %all-reduce.12.cloned.1.call-start = ((), (), s32[]{:S(2)}) async-start(), calls=%async_computation.18 | async-start | bytes 16777216
  702.8 5.2 copy-start.13
  702.8 299.7 %reduce-scatter.10.cloned.1.call-start = ((), (), s32[]{:S(2)}) async-start(), calls=%async_computation.13 | async-start | bytes 2228224 | tf_op jit(solution)/shard_map/reduce_scatter | solution.py:261
  707.9 403.2 %reduce-scatter.14.cloned.1.call-start = ((), (), s32[]{:S(2)}) async-start(), calls=%async_computation.15 | async-start | bytes 8912896 | tf_op jit(solution)/shard_map/reduce_scatter | solution.py:176
  717.8 502.8 %reduce-scatter.12.cloned.1.call-start = ((), (), s32[]{:S(2)}) async-start(), calls=%async_computation.14 | async-start | bytes 8912896 | tf_op jit(solution)/shard_map/reduce_scatter | solution.py:175
  726.8 2.0 copy-start.17
  726.9 36.1 %copy-start.35 = (f32[1024]{0:T(1024)S(1)}, f32[1024]{0:T(1024)}, u32[]{:S(2)}) copy-start(f32[1024]{0:T(1024)} %get-tuple-element.566) | copy-start | bytes 12292
  726.9 36.1 %copy-start.34 = (f32[1024]{0:T(1024)S(1)}, f32[1024]{0:T(1024)}, u32[]{:S(2)}) copy-start(f32[1024]{0:T(1024)} %get-tuple-element.573) | copy-start | bytes 12292
  726.9 36.1 %copy-start.32 = (f32[1024]{0:T(1024)S(1)}, f32[1024]{0:T(1024)}, u32[]{:S(2)}) copy-start(f32[1024]{0:T(1024)} %get-tuple-element.672) | copy-start | bytes 12292
  726.9 36.1 %copy-start.33 = (f32[1024]{0:T(1024)S(1)}, f32[1024]{0:T(1024)}, u32[]{:S(2)}) copy-start(f32[1024]{0:T(1024)} %get-tuple-element.689) | copy-start | bytes 12292
  726.9 36.1 %copy-start.38 = (f32[2048]{0:T(1024)S(1)}, f32[2048]{0:T(1024)}, u32[]{:S(2)}) copy-start(f32[2048]{0:T(1024)} %get-tuple-element.670) | copy-start | bytes 24580
  726.9 102.0 %copy-start.39 = (f32[1024]{0:T(1024)S(1)}, f32[1024]{0:T(1024)}, u32[]{:S(2)}) copy-start(f32[1024]{0:T(1024)} %param.35) | copy-start | bytes 12292
  (18 other events, 23.9 us)
Sparse Core Ops, SparseCore 0:
  10.3 48.1 all-gather.10
  64.7 53.8 all-gather.18
  120.2 53.3 all-gather.20
  175.6 36.6 all-gather.12
  272.9 44.3 all-reduce.7
  319.6 50.6 all-gather.14
  372.8 49.0 all-gather.16
  437.1 44.2 all-reduce.9
  574.2 52.0 reduce-scatter.7
  628.5 51.7 reduce-scatter.5
  686.2 74.1 all-reduce.13
  764.5 172.2 all-reduce.11
  941.0 61.4 reduce-scatter.9
  1007.5 103.5 reduce-scatter.13
  1116.2 104.3 reduce-scatter.11
where the time goes:
time: 1230 us
  waiting for transfers between devices  775 us (63%)
  matrix products  205 us (17%)
  blocking collectives  92.4 us (8%)
  other arithmetic  76.9 us (6%)
  local copies, waits for them, and re-layouts  60.1 us (5%)
  between operations  15.5 us (1%)
    reduce_scatter x1, waiting for transfers between devices, per_device(): lax.psum_scatter(up_term, ('shard', 'ctx'), scatter_dimension=0, tiled=True)  109 us
    reduce_scatter x1, waiting for transfers between devices, per_device(): lax.psum_scatter(down_term, ('shard', 'ctx'), scatter_dimension=1, tiled=...  109 us
    unnamed x16, waiting for transfers between devices  107 us
    psum x1, blocking collectives, per_device(): lax.psum((bias_qv_part, out_bias_part, up_bias_part, down_bias_part, gain...  65.9 us
    reduce_scatter x1, waiting for transfers between devices, per_device(): lax.psum_scatter(out_term, ('shard', 'ctx'), scatter_dimension=1, tiled=T...  63.8 us
    reduce_scatter x1, waiting for transfers between devices, per_device(): lax.psum_scatter(key_terms.reshape(group_rows, head_width).astype(jnp.bfl...  54 us
    all_gather x1, waiting for transfers between devices, per_device(): lax.all_gather(w_up, ('shard', 'ctx'), axis=0, tiled=True)  50.4 us
    dot_general x10, matrix products, block_scores(): jnp.einsum('qhd,khd->hqk', query_heads, key_heads, preferred_element_type...  49.1 us
  transfers between devices with their start and end apart: 15, of which 13 were waited for; matrix products, arithmetic and copies ran while one was open for 18% of the time, Pallas kernels for 0%

commit v1 on v0

--- a/solution.py
+++ b/solution.py
@@ -3,6 +3,7 @@
 import jax.numpy as jnp
 from jax import lax
 from jax.sharding import PartitionSpec as P
+from jax.lax import psum
 
 HEADS = 16
 HD = 64
@@ -273,9 +274,12 @@
         [jnp.sum(grad_norm_one * normed_one, axis=0), jnp.sum(grad_norm_two * normed_two, axis=0)]
     )
     shift_part = jnp.stack([jnp.sum(grad_norm_one, axis=0), jnp.sum(grad_norm_two, axis=0)])
-    grad_b_qv, grad_b_out, grad_b_up, grad_b_down, grad_gain, grad_shift = lax.psum(
-        (bias_qv_part, out_bias_part, up_bias_part, down_bias_part, gain_part, shift_part),
-        ("shard", "ctx"),
+    grad_b_qv, grad_b_out, grad_b_up, grad_b_down, grad_gain, grad_shift = psum(
+        psum(
+            (bias_qv_part, out_bias_part, up_bias_part, down_bias_part, gain_part, shift_part),
+            "ctx",
+        ),
+        "shard",
     )
     return (
         result,

time: 1230 us -> 1230 us (level)
  blocking collectives: 92.4 us -> 59 us
  waiting for transfers between devices: 775 us -> 807 us
    psum x1 -> x2, blocking collectives: 65.9 us -> 32.4 us  [the longest x1 20.4 us: per_device(): psum((bias_qv_part, out_bias_part, up_bias_part, down_bias_part, gain_par...]
    unnamed x16, waiting for transfers between devices: 107 us -> 138 us
where the time goes in v1:
time: 1230 us
  waiting for transfers between devices  807 us (66%)
  matrix products  205 us (17%)
  other arithmetic  76.9 us (6%)
  local copies, waits for them, and re-layouts  60.1 us (5%)
  blocking collectives  59 us (5%)
  between operations  15.5 us (1%)
    unnamed x16, waiting for transfers between devices  138 us
    reduce_scatter x1, waiting for transfers between devices, per_device(): lax.psum_scatter(up_term, ('shard', 'ctx'), scatter_dimension=0, tiled=True)  109 us
    reduce_scatter x1, waiting for transfers between devices, per_device(): lax.psum_scatter(down_term, ('shard', 'ctx'), scatter_dimension=1, tiled=...  109 us
    reduce_scatter x1, waiting for transfers between devices, per_device(): lax.psum_scatter(out_term, ('shard', 'ctx'), scatter_dimension=1, tiled=T...  63.7 us
    reduce_scatter x1, waiting for transfers between devices, per_device(): lax.psum_scatter(key_terms.reshape(group_rows, head_width).astype(jnp.bfl...  54 us
    all_gather x1, waiting for transfers between devices, per_device(): lax.all_gather(w_up, ('shard', 'ctx'), axis=0, tiled=True)  50.4 us
    dot_general x10, matrix products, block_scores(): jnp.einsum('qhd,khd->hqk', query_heads, key_heads, preferred_element_type...  49.1 us
    all_gather x1, waiting for transfers between devices, per_device(): lax.all_gather(w_qkv, ('shard', 'ctx'), axis=1, tiled=True)  46.8 us
  transfers between devices with their start and end apart: 15, of which 13 were waited for; matrix products, arithmetic and copies ran while one was open for 18% of the time, Pallas kernels for 0%

profile of v1, /device:TPU:0, one launch (start us, length us, event | category | flops | bytes accessed | tf_op | source)
XLA Modules:
  0.0 1225.7 jit_solution(9680974198860835281)
XLA Ops:
  11.7 46.8 %all-gather.11.cloned.1.call-done = bf16[3,1024,512]{2,1,0:T(8,128)(2,1)} async-done(((bf16[3,64,512]{2,1,0:T(8,128)(2,1)}), bf16[3,1024,512]{2,1,0:T(8,128)(2,1)}) %all-gather.11.cloned.1.call-update) | async-done | bytes 3145744 | tf_op jit(solution)/shard_map/all_gather | solution.py:80
  58.5 4.7 fusion.83
  68.2 13.2 %all-gather.2 = s32[4,1,640]{2,1,0:T(1,128)S(1)} all-gather(s32[1,1,640]{2,1,0:T(1,128)S(1)} %reshape.676), channel_id=1, replica_groups=mesh['shard'=4,'ctx'=4,'tp'=2] {'ctx'}, dimensions={0}, use_global_device_ids=true | all-gather | bytes 12800 | tf_op jit(solution)/shard_map/all_gather | solution.py:84
  81.5 13.3 %all-gather.3 = s32[4,1,640]{2,1,0:T(1,128)S(1)} all-gather(s32[1,1,640]{2,1,0:T(1,128)S(1)} %reshape.678), channel_id=1, replica_groups=mesh['shard'=4,'ctx'=4,'tp'=2] {'ctx'}, dimensions={0}, use_global_device_ids=true | all-gather | bytes 12800 | tf_op jit(solution)/shard_map/all_gather | solution.py:85
  94.9 32.4 %select_select_fusion = (s32[640]{0:T(1024)S(1)}, s32[640]{0:T(1024)S(1)}) fusion(s32[]{:T(128)} %bitcast.57, s32[]{:T(128)} %bitcast.56, s32[]{:T(128)} %bitcast.55, s32[]{:T(128)} %bitcast.54, s32[]{:T(128)} %bitcast.53, s32[]{:T(128)} %bitcast.52, s32[]{:T(128)} %bitcast.51, s32[]{:T(128)} %bitcast.50, s32[]{:T(128)} %bitcast.49, s32[]{:T(128)} %bitcast.48, ...), kind=kLoop, calls=%fused_computation.139 | loop fusion | flops 139520 | bytes 7888 | tf_op jit(solution)/shard_map/jit(_take)/select_n | solution.py:31
  127.3 7.1 reshape.547
  139.0 34.5 %all-gather.21.cloned.1.call-done = bf16[1,2560,512]{1,2,0:T(8,128)(2,1)} async-done(((bf16[1,640,512]{1,2,0:T(8,128)(2,1)}), bf16[1,2560,512]{1,2,0:T(8,128)(2,1)}) %all-gather.21.cloned.1.call-update) | async-done | bytes 2621456 | tf_op jit(solution)/shard_map/all_gather | solution.py:97
  173.6 7.0 reshape.550
  180.6 4.7 copy.61
  185.3 41.6 %while.39 = (s32[]{:T(128)}, f32[8,640]{1,0:T(8,128)S(1)}, f32[8,640]{1,0:T(8,128)S(1)}, s32[5,512]{1,0:T(8,128)S(1)}, s32[640]{0:T(1024)S(1)}, /*index=5*/s32[6...) while((s32[]{:T(128)}, f32[8,640]{1,0:T(8,128)S(1)}, ...), condition=%wide.region_5.7_spmd.clone, body=%wide.region_2.6_spmd.clone.sunk | while | flops 367354912 | bytes 27360004 | solution.py:123
  185.9 4.8 select_reduce_fusion.2
  194.2 4.7 select_reduce_fusion.2
  202.5 4.8 select_reduce_fusion.2
  210.9 4.8 select_reduce_fusion.2
  219.2 4.8 select_reduce_fusion.2
  226.9 40.9 %while.40 = (s32[]{:T(128)}, f32[640,8,64]{0,2,1:T(8,128)}, bf16[5,512,8,64]{1,3,2,0:T(8,128)(2,1)}, s32[5,512]{1,0:T(8,128)S(1)}, s32[640]{0:T(1024)S(1)}, /*in...) while((s32[]{:T(128)}, f32[640,8,64]{0,2,1:T(8,128)}, ...), condition=%wide.region_7.9_spmd.clone, body=%wide.region_6.8_spmd.clone.sunk | while | flops 693043264 | bytes 7672046 | solution.py:137
  227.8 7.2 fusion.154
  235.6 7.6 fusion.154
  243.8 7.6 fusion.154
  252.0 7.6 fusion.154
  260.2 7.6 fusion.154
  274.1 43.2 %all-reduce.9.cloned.1.call-done = bf16[640,1024]{1,0:T(8,128)(2,1)} async-done(((bf16[640,1024]{1,0:T(8,128)(2,1)}), bf16[640,1024]{1,0:T(8,128)(2,1)}) %all-reduce.9.cloned.1.call-update) | async-done | bytes 1310736 | tf_op jit(solution)/shard_map/psum | solution.py:144
  319.9 50.4 %all-gather.15.cloned.1.call-done = bf16[1024,2048]{1,0:T(8,128)(2,1)} async-done(((bf16[64,2048]{1,0:T(8,128)(2,1)}), bf16[1024,2048]{1,0:T(8,128)(2,1)}) %all-gather.15.cloned.1.call-update) | async-done | bytes 4194320 | tf_op jit(solution)/shard_map/all_gather | solution.py:154
  370.3 7.7 fusion.95
  378.1 43.8 %all-gather.17.cloned.1.call-done = bf16[2048,1024]{0,1:T(8,128)(2,1)} async-done(((bf16[2048,64]{0,1:T(8,128)(2,1)}), bf16[2048,1024]{0,1:T(8,128)(2,1)}) %all-gather.17.cloned.1.call-update) | async-done | bytes 4194320 | tf_op jit(solution)/shard_map/all_gather | solution.py:155
  421.8 9.6 convert_reduce_fusion
  437.1 44.3 %all-reduce.11.cloned.1.call-done = bf16[640,1024]{1,0:T(8,128)(2,1)} async-done(((bf16[640,1024]{1,0:T(8,128)(2,1)}), bf16[640,1024]{1,0:T(8,128)(2,1)}) %all-reduce.11.cloned.1.call-update) | async-done | bytes 1310736 | tf_op jit(solution)/shard_map/psum | solution.py:179
  489.5 80.3 %while.41 = (s32[]{:T(128)}, f32[640,8,64]{0,2,1:T(8,128)S(1)}, bf16[5,512,512]{1,2,0:T(8,128)(2,1)}, bf16[5,512,512]{1,2,0:T(8,128)(2,1)}, bf16[5,512,8,64]{1,3...) while((s32[]{:T(128)}, f32[640,8,64]{0,2,1:T(8,128)S(1)}, ...), condition=%wide.region_16.18_spmd.clone, body=%wide.region_15.17_spmd.clone.sunk | while | flops 1708392448 | bytes 60513056 | solution.py:229
  490.1 5.1 fusion.165
  506.1 5.1 fusion.165
  522.2 5.1 fusion.165
  538.3 5.1 fusion.165
  554.3 5.1 fusion.165
  579.3 8.7 convolution_convert_fusion.1
  588.5 37.9 %reduce-scatter.8.cloned.1.call-done = bf16[640,512]{1,0:T(8,128)(2,1)} async-done(((bf16[2560,512]{1,0:T(8,128)(2,1)}), bf16[640,512]{1,0:T(8,128)(2,1)}) %reduce-scatter.8.cloned.1.call-update) | async-done | bytes 655376 | tf_op jit(solution)/shard_map/reduce_scatter | solution.py:241
  626.4 54.0 %reduce-scatter.6.cloned.1.call-done = bf16[640,512]{1,0:T(8,128)(2,1)} async-done(((bf16[2560,512]{1,0:T(8,128)(2,1)}), bf16[640,512]{1,0:T(8,128)(2,1)}) %reduce-scatter.6.cloned.1.call-update) | async-done | bytes 655376 | tf_op jit(solution)/shard_map/reduce_scatter | solution.py:235
  680.4 5.6 bitcast_convert_fusion
  687.5 5.8 convolution_bitcast_fusion
  693.3 9.4 copy.68
  708.0 9.7 fusion.96
  719.0 7.7 fusion.94
  728.9 31.6 %all-reduce.15.cloned.1.call-done = (bf16[640,1024]{1,0:T(8,128)(2,1)}, bf16[640,1024]{1,0:T(8,128)(2,1)}) async-done(((bf16[640,1024]{1,0:T(8,128)(2,1)}, bf16[640,1024]{1,0:T(8,128)(2,1)}), (bf16[640,1024]{1,0:T(8,128)(2,1)}, bf16[640,1024]{1,0:T(8,128)(2,1)})) %all-reduce.15.cloned.1.call-update) | async-done | bytes 2621456 | tf_op jit(solution)/shard_map/psum | solution.py:163
  763.1 20.4 %all-reduce.1 = (f32[2,512]{1,0:T(2,128)S(1)}, f32[1024]{0:T(1024)S(1)}, f32[2048]{0:T(1024)S(1)}, f32[1024]{0:T(1024)S(1)}, f32[2,1024]{1,0:T(2,128)S(1)}, /*index=5*/f32[2,1024]{1,0:T(2,128)S(1)}) all-reduce(f32[2,512]{1,0:T(2,128)S(1)} %pad_maximum_fusion.6, ...), channel_id=1, replica_groups=mesh['shard'=4,'ctx'=4,'tp'=2] {'ctx'}, use_global_device_ids=true, to_apply=%region_25.27 | all-reduce | flops 9216 | bytes 73728 | tf_op jit(solution)/shard_map/psum | solution.py:278
  783.4 12.0 all-reduce.2
  800.0 135.1 %all-reduce.13.cloned.1.call-done = f32[3,1024,512]{2,0,1:T(4,128)} async-done(((f32[3,1024,512]{2,0,1:T(4,128)}), f32[3,1024,512]{2,0,1:T(4,128)}) %all-reduce.13.cloned.1.call-update) | async-done | bytes 6291472
  937.1 63.7 %reduce-scatter.10.cloned.1.call-done = f32[512,64]{0,1:T(8,128)} async-done(((f32[512,1024]{0,1:T(8,128)}), f32[512,64]{0,1:T(8,128)}) %reduce-scatter.10.cloned.1.call-update) | async-done | bytes 131088 | tf_op jit(solution)/shard_map/reduce_scatter | solution.py:262
  1000.9 108.6 %reduce-scatter.14.cloned.1.call-done = f32[2048,64]{0,1:T(8,128)} async-done(((f32[2048,1024]{0,1:T(8,128)}), f32[2048,64]{0,1:T(8,128)}) %reduce-scatter.14.cloned.1.call-update) | async-done | bytes 524304 | tf_op jit(solution)/shard_map/reduce_scatter | solution.py:177
  1109.5 109.4 %reduce-scatter.12.cloned.1.call-done = f32[64,2048]{1,0:T(8,128)} async-done(((f32[1024,2048]{1,0:T(8,128)}), f32[64,2048]{1,0:T(8,128)}) %reduce-scatter.12.cloned.1.call-update) | async-done | bytes 524304 | tf_op jit(solution)/shard_map/reduce_scatter | solution.py:176
  (298 shorter events, 139.8 us)
Async XLA Ops:
  7.2 51.3 %copy-start = (bf16[640,1024]{1,0:T(8,128)(2,1)S(1)}, bf16[640,1024]{1,0:T(8,128)(2,1)}, u32[]{:S(2)}) copy-start(bf16[640,1024]{1,0:T(8,128)(2,1)} %param.23) | copy-start | bytes 3932164
  7.2 4.3 copy-start.40
  7.2 4.4 copy-start.36
  7.2 4.4 copy-start.37
  7.2 51.2 %all-gather.11.cloned.1.call-start = ((), (), s32[]{:S(2)}) async-start(), calls=%async_computation.5 | async-start | bytes 3342336 | tf_op jit(solution)/shard_map/all_gather | solution.py:80
  8.0 119.3 %all-gather.19.cloned.1.call-start = ((), (), s32[]{:S(2)}) async-start(), calls=%async_computation.16 | async-start | bytes 3276800 | tf_op jit(solution)/shard_map/all_gather | solution.py:98
  9.6 48.8 %copy-start.20 = (f32[640]{0:T(1024)}, f32[640]{0:T(1024)S(1)}, u32[]{:S(2)}) copy-start(f32[640]{0:T(1024)S(1)} %broadcast_multiply_fusion.5) | copy-start | bytes 7684
  11.5 51.7 %copy-start.24 = (f32[640]{0:T(1024)}, f32[640]{0:T(1024)S(1)}, u32[]{:S(2)}) copy-start(f32[640]{0:T(1024)S(1)} %add_rsqrt_fusion.1) | copy-start | bytes 7684
  11.6 51.6 %copy-start.26 = (f32[1,1024]{1,0:T(1,128)}, f32[1,1024]{1,0:T(1,128)S(1)}, u32[]{:S(2)}) copy-start(f32[1,1024]{1,0:T(1,128)S(1)} %get-tuple-element.698) | copy-start | bytes 12292
  11.6 473.8 %copy-start.30 = (f32[1,1024]{1,0:T(1,128)}, f32[1,1024]{1,0:T(1,128)S(1)}, u32[]{:S(2)}) copy-start(f32[1,1024]{1,0:T(1,128)S(1)} %get-tuple-element.699) | copy-start | bytes 12292
  11.6 51.6 %copy-start.43 = (f32[1,1024]{1,0:T(1,128)}, f32[1,1024]{1,0:T(1,128)S(1)}, u32[]{:S(2)}) copy-start(f32[1,1024]{1,0:T(1,128)S(1)} %get-tuple-element.700) | copy-start | bytes 12292
  11.6 358.7 %copy-start.41 = (f32[1,1024]{1,0:T(1,128)}, f32[1,1024]{1,0:T(1,128)S(1)}, u32[]{:S(2)}) copy-start(f32[1,1024]{1,0:T(1,128)S(1)} %get-tuple-element.701) | copy-start | bytes 12292
  63.2 2.8 copy-start.11
  63.2 4.9 copy-start.8
  63.3 4.9 copy-start.14
  64.6 108.9 %all-gather.21.cloned.1.call-start = ((), (), s32[]{:S(2)}) async-start(), calls=%async_computation.17 | async-start | bytes 3276800 | tf_op jit(solution)/shard_map/all_gather | solution.py:97
  65.4 203.9 %all-gather.13.cloned.1.call-start = ((), (), s32[]{:S(2)}) async-start(), calls=%async_computation.6 | async-start | bytes 1114112 | tf_op jit(solution)/shard_map/all_gather | solution.py:81
  65.9 251.3 %all-reduce.9.cloned.1.call-start = ((), (), s32[]{:S(2)}) async-start(), calls=%async_computation.7 | async-start | bytes 2621440 | tf_op jit(solution)/shard_map/psum | solution.py:144
  269.2 4.1 copy-start.9
  269.3 48.0 %copy-start.18 = (f32[1024]{0:T(1024)S(1)}, f32[1024]{0:T(1024)}, u32[]{:S(2)}) copy-start(f32[1024]{0:T(1024)} %param.31) | copy-start | bytes 12292
  272.7 97.6 %all-gather.15.cloned.1.call-start = ((), (), s32[]{:S(2)}) async-start(), calls=%async_computation.8 | async-start | bytes 4456448 | tf_op jit(solution)/shard_map/all_gather | solution.py:154
  273.3 148.5 %all-gather.17.cloned.1.call-start = ((), (), s32[]{:S(2)}) async-start(), calls=%async_computation.9 | async-start | bytes 4456448 | tf_op jit(solution)/shard_map/all_gather | solution.py:155
  274.1 207.4 %all-reduce.11.cloned.1.call-start = ((), (), s32[]{:S(2)}) async-start(), calls=%async_computation.10 | async-start | bytes 2621440 | tf_op jit(solution)/shard_map/psum | solution.py:179
  319.2 166.2 %copy-start.22 = (f32[640]{0:T(1024)}, f32[640]{0:T(1024)S(1)}, u32[]{:S(2)}) copy-start(f32[640]{0:T(1024)S(1)} %broadcast_multiply_fusion.4) | copy-start | bytes 7684
  319.9 165.5 %copy-start.28 = (f32[640]{0:T(1024)}, f32[640]{0:T(1024)S(1)}, u32[]{:S(2)}) copy-start(f32[640]{0:T(1024)S(1)} %add_rsqrt_fusion) | copy-start | bytes 7684
  370.3 51.5 %copy-start.47 = (f32[2048]{0:T(1024)S(1)}, f32[2048]{0:T(1024)}, u32[]{:S(2)}) copy-start(f32[2048]{0:T(1024)} %param.33) | copy-start | bytes 24580
  421.8 11.1 copy-start.45
  437.0 189.4 %reduce-scatter.8.cloned.1.call-start = ((), (), s32[]{:S(2)}) async-start(), calls=%async_computation.12 | async-start | bytes 3276800 | tf_op jit(solution)/shard_map/reduce_scatter | solution.py:241
  481.4 4.0 copy-start.4
  481.4 4.0 copy-start.7
  481.4 4.0 copy-start.12
  485.4 2.6 copy-start.6
  485.4 2.5 copy-start.15
  574.1 106.2 %reduce-scatter.6.cloned.1.call-start = ((), (), s32[]{:S(2)}) async-start(), calls=%async_computation.11 | async-start | bytes 3276800 | tf_op jit(solution)/shard_map/reduce_scatter | solution.py:235
  578.6 181.8 %all-reduce.15.cloned.1.call-start = ((), (), s32[]{:S(2)}) async-start(), calls=%async_computation.19 | async-start | bytes 5242880 | tf_op jit(solution)/shard_map/psum | solution.py:163
  680.4 5.8 copy-start.46
  686.1 249.0 %all-reduce.13.cloned.1.call-start = ((), (), s32[]{:S(2)}) async-start(), calls=%async_computation.18 | async-start | bytes 16777216
  702.8 5.2 copy-start.13
  702.8 298.1 %reduce-scatter.10.cloned.1.call-start = ((), (), s32[]{:S(2)}) async-start(), calls=%async_computation.13 | async-start | bytes 2228224 | tf_op jit(solution)/shard_map/reduce_scatter | solution.py:262
  707.9 401.6 %reduce-scatter.14.cloned.1.call-start = ((), (), s32[]{:S(2)}) async-start(), calls=%async_computation.15 | async-start | bytes 8912896 | tf_op jit(solution)/shard_map/reduce_scatter | solution.py:177
  717.7 501.2 %reduce-scatter.12.cloned.1.call-start = ((), (), s32[]{:S(2)}) async-start(), calls=%async_computation.14 | async-start | bytes 8912896 | tf_op jit(solution)/shard_map/reduce_scatter | solution.py:176
  726.8 2.0 copy-start.17
  726.8 36.2 %copy-start.35 = (f32[1024]{0:T(1024)S(1)}, f32[1024]{0:T(1024)}, u32[]{:S(2)}) copy-start(f32[1024]{0:T(1024)} %get-tuple-element.566) | copy-start | bytes 12292
  726.8 36.2 %copy-start.34 = (f32[1024]{0:T(1024)S(1)}, f32[1024]{0:T(1024)}, u32[]{:S(2)}) copy-start(f32[1024]{0:T(1024)} %get-tuple-element.573) | copy-start | bytes 12292
  726.8 36.2 %copy-start.32 = (f32[1024]{0:T(1024)S(1)}, f32[1024]{0:T(1024)}, u32[]{:S(2)}) copy-start(f32[1024]{0:T(1024)} %get-tuple-element.678) | copy-start | bytes 12292
  726.8 36.2 %copy-start.33 = (f32[1024]{0:T(1024)S(1)}, f32[1024]{0:T(1024)}, u32[]{:S(2)}) copy-start(f32[1024]{0:T(1024)} %get-tuple-element.695) | copy-start | bytes 12292
  726.8 36.2 %copy-start.38 = (f32[2048]{0:T(1024)S(1)}, f32[2048]{0:T(1024)}, u32[]{:S(2)}) copy-start(f32[2048]{0:T(1024)} %get-tuple-element.676) | copy-start | bytes 24580
  726.9 68.6 %copy-start.39 = (f32[1024]{0:T(1024)S(1)}, f32[1024]{0:T(1024)}, u32[]{:S(2)}) copy-start(f32[1024]{0:T(1024)} %param.35) | copy-start | bytes 12292
  (18 other events, 24.0 us)
Sparse Core Ops, SparseCore 0:
  10.3 48.1 all-gather.10
  64.7 53.8 all-gather.18
  120.2 53.3 all-gather.20
  175.6 36.6 all-gather.12
  272.8 44.3 all-reduce.8
  319.6 50.6 all-gather.14
  372.8 49.0 all-gather.16
  437.1 44.2 all-reduce.10
  574.2 52.0 reduce-scatter.7
  628.5 51.7 reduce-scatter.5
  686.2 74.2 all-reduce.14
  764.5 170.5 all-reduce.12
  939.4 61.3 reduce-scatter.9
  1005.9 103.5 reduce-scatter.13
  1114.5 104.3 reduce-scatter.11
